TPU v7x, 256 devices: a whole 4x4x8 slice. The times are simulated.
256 devices in a mesh: space: 64 (over z, y, core), tm: 4 (over x).
Axes of the slice: x: 4, y: 4, z: 8, core: 2. Of those that a mesh axis runs over, the one named last changes fastest.
Arguments:
- snapshots: bfloat16 [256, 524288], P('tm', 'space'), may hold values from -75 to 75
- prior_basis: bfloat16 [256, 524288], P('tm', 'space'), may hold values from -75 to 75
- mass_factor: bfloat16 [7, 64, 524288], P(None, None, 'space'), may hold values from -1 to 3.2, as said below
- neighbours: int32 [8192, 7], P('space'), may hold values from 0 to 8191, as said below
Outputs:
- merged_basis: bfloat16 [64, 524288], P(None, ('space', 'tm'))
- merged_weighted: bfloat16 [64, 524288], P(None, ('space', 'tm'))
Inputs may be any that keep to these rules, and one draw needn't show every extreme that they name: `mass_factor`: factor entries; the diagonal of each block's own coupling lies in 1.5 to 3. neighbours[i, 0] = i; every entry lies within 8 blocks of i; in every draw some entries lie exactly 8 blocks below and above their block.
All inputs are finite; a program needn't handle non-finite values.
Results may differ from a plain program's by a relative error of at most 0.018.
Values may be sent and summed in bfloat16 or wider, within the bound.
A program may use at most 128 MiB of HBM per device.

v0:
```python
import jax
import jax.numpy as jnp
from jax import lax
from jax.sharding import PartitionSpec as P

BLOCK_DOFS = 64
RANK = 64
NEIGHBOURS = 7
REACH = 8
SUBSPACE_STEPS = 3
LOCAL_BLOCKS = 128


def padded(block, sides, width):
    for axis, dim in sides:
        count = lax.axis_size(axis)
        forward = [(i, i + 1) for i in range(count - 1)]
        backward = [(target, source) for source, target in forward]
        low = lax.ppermute(
            lax.slice_in_dim(block, block.shape[dim] - width, None, axis=dim), axis, forward
        )
        high = lax.ppermute(lax.slice_in_dim(block, 0, width, axis=dim), axis, backward)
        block = jnp.concatenate([low, block, high], axis=dim)
    return block


def partner(block, axis, bit):
    count = lax.axis_size(axis)
    route = []
    for low in range(count):
        high = low | 1 << bit
        if high != low and high < count:
            route += [(low, high), (high, low)]
    return lax.ppermute(block, axis, route)


def weigh_rows(stacked, mass_factor, local_index):
    columns = stacked.shape[0]
    widened = padded(stacked, (("space", 1),), REACH * BLOCK_DOFS)
    blocks = widened.reshape(columns, -1, BLOCK_DOFS)
    picked = jnp.take(blocks, local_index, axis=1)
    factor = mass_factor.reshape(NEIGHBOURS, BLOCK_DOFS, -1, BLOCK_DOFS)
    result = jnp.einsum("cbkq,kqbr->cbr", picked, factor, preferred_element_type=jnp.float32)
    return result.reshape(columns, -1).astype(jnp.bfloat16)


def compress(gram_total):
    highest = lax.Precision.HIGHEST
    order_size = gram_total.shape[0]
    weights = jnp.eye(order_size, RANK, dtype=jnp.float32)
    for repeat in range(SUBSPACE_STEPS):
        product = jnp.dot(gram_total, weights, precision=highest)
        inner_gram = jnp.dot(
            product.T, jnp.dot(gram_total, product, precision=highest), precision=highest
        )
        scales = jnp.sqrt(jnp.diagonal(inner_gram))
        factor_lower = jnp.linalg.cholesky(inner_gram / (scales[:, None] * scales[None, :]))
        normed = product / scales[None, :]
        weights = lax.linalg.triangular_solve(
            factor_lower, normed, left_side=False, lower=True, transpose_a=True
        )
    product = jnp.dot(gram_total, weights, precision=highest)
    lengths = jnp.sqrt(jnp.sum(product * product, axis=0) + 1e-06)
    return (weights * lengths[None, :]).astype(jnp.bfloat16)


def coefficients_of(weighted):
    local_gram = jnp.dot(weighted, weighted.T, preferred_element_type=jnp.float32)
    return compress(lax.psum(local_gram, "space"))


def apply_coefficients(coefficients, stacked, weighted):
    basis = jnp.dot(coefficients.T, stacked, preferred_element_type=jnp.float32).astype(
        jnp.bfloat16
    )
    weighted_basis = jnp.dot(coefficients.T, weighted, preferred_element_type=jnp.float32).astype(
        jnp.bfloat16
    )
    return (basis, weighted_basis)


def ordered(upper_half, own_rows, partner_rows):
    lower_part = jnp.where(upper_half, partner_rows, own_rows)
    upper_part = jnp.where(upper_half, own_rows, partner_rows)
    return jnp.concatenate([lower_part, upper_part], axis=0)


def shards(snapshots, prior_basis, mass_factor, neighbours):
    local_index = neighbours - (lax.axis_index("space") * LOCAL_BLOCKS - REACH)
    stacked = jnp.concatenate([prior_basis, snapshots], axis=0)
    weighted = weigh_rows(stacked, mass_factor, local_index)
    basis, weighted_basis = apply_coefficients(coefficients_of(weighted), stacked, weighted)
    member = lax.axis_index("tm")
    for level_bit in range(lax.axis_size("tm").bit_length() - 1):
        upper_half = member // (1 << level_bit) % 2 == 1
        partner_weighted = partner(weighted_basis, "tm", level_bit)
        weighted = ordered(upper_half, weighted_basis, partner_weighted)
        coefficients = coefficients_of(weighted)
        partner_rows = partner(basis, "tm", level_bit)
        stacked = ordered(upper_half, basis, partner_rows)
        basis, weighted_basis = apply_coefficients(coefficients, stacked, weighted)
    share_width = basis.shape[1] // lax.axis_size("tm")
    basis_share = lax.dynamic_slice_in_dim(basis, member * share_width, share_width, 1)
    weighted_share = lax.dynamic_slice_in_dim(weighted_basis, member * share_width, share_width, 1)
    return (basis_share, weighted_share)


def solution(mesh):
    return jax.shard_map(
        shards,
        mesh=mesh,
        in_specs=(P("tm", "space"), P("tm", "space"), P(None, None, "space"), P("space", None)),
        out_specs=(P(None, ("space", "tm")), P(None, ("space", "tm"))),
        check_vma=False,
    )
```

profile of v0, /device:TPU:1, one launch (start us, length us, event | category | flops | bytes accessed | tf_op | source)
XLA Modules:
  0.0 817.4 jit_solution(14722766213442780236)
XLA Ops:
  19.5 20.9 %reshape.97 = bf16[7,64,128,64]{3,2,1,0:T(8,128)(2,1)} reshape(bf16[7,64,8192]{2,1,0:T(8,128)(2,1)} %param.9) | data formatting | bytes 14680064 | tf_op jit(solution)/shard_map/reshape | solution.py:42
  40.5 6.7 pad_maximum_fusion
  47.1 22.8 %gather_fusion = bf16[896,128,64]{1,2,0:T(8,128)(2,1)} fusion(bf16[128,144,64]{0,2,1:T(8,128)(2,1)S(1)} %bitcast.178, s32[1024]{0:T(1024)S(1)} %pad_clamp_fusion), kind=kCustom, calls=%fused_computation | custom fusion | bytes 29363712 | tf_op jit(solution)/shard_map/jit(_take)/gather | solution.py:41
  69.9 29.0 %bitcast_convert_fusion = bf16[128,128,64]{1,2,0:T(8,128)(2,1)S(1)} fusion(bf16[128,7,128,64]{2,3,1,0:T(8,128)(2,1)} %bitcast.179, pred[128,7]{1,0:T(8,128)(4,1)S(1)} %copy.29, bf16[7,64,128,64]{3,2,1,0:T(8,128)(2,1)} %reshape.97), kind=kOutput, calls=%fused_computation.20 | convolution fusion | flops 947912704 | bytes 24118144 | tf_op jit(solution)/shard_map/cbkq,kqbr->cbr/dot_general | solution.py:43
  100.4 174.6 %all-reduce.4.cloned.1.call-done = f32[128,128]{1,0:T(8,128)} async-done(((f32[128,128]{1,0:T(8,128)}), f32[128,128]{1,0:T(8,128)}) %all-reduce.4.cloned.1.call-update) | async-done | bytes 65552 | tf_op jit(solution)/shard_map/psum | solution.py:69
  278.5 5.8 cholesky.149
  285.7 4.9 custom-call.31
  294.4 5.8 cholesky.160
  308.6 5.8 cholesky.171
  315.8 4.9 custom-call.33
  323.5 23.1 %collective-permute-done.2 = bf16[64,8192]{1,0:T(8,128)(2,1)S(1)} collective-permute-done((bf16[64,8192]{1,0:T(8,128)(2,1)S(1)}, bf16[64,8192]{1,0:T(8,128)(2,1)S(1)}, u32[]{:S(2)}, u32[]{:S(2)}) %collective-permute-start.2) | collective-permute-done | bytes 1048608 | tf_op jit(solution)/shard_map/ppermute | solution.py:34
  354.2 163.1 %all-reduce.6.cloned.1.call-done = f32[128,128]{1,0:T(8,128)} async-done(((f32[128,128]{1,0:T(8,128)}), f32[128,128]{1,0:T(8,128)}) %all-reduce.6.cloned.1.call-update) | async-done | bytes 65552 | tf_op jit(solution)/shard_map/psum | solution.py:69
  520.9 5.8 cholesky.182
  528.1 4.9 custom-call.34
  536.8 5.8 cholesky.193
  551.0 5.8 cholesky.204
  558.2 4.9 custom-call.36
  570.6 20.7 %collective-permute-done.3 = bf16[64,8192]{1,0:T(8,128)(2,1)S(1)} collective-permute-done((bf16[64,8192]{1,0:T(8,128)(2,1)S(1)}, bf16[64,8192]{1,0:T(8,128)(2,1)S(1)}, u32[]{:S(2)}, u32[]{:S(2)}) %collective-permute-start.3) | collective-permute-done | bytes 1048608 | tf_op jit(solution)/shard_map/ppermute | solution.py:34
  592.9 21.1 %collective-permute-done.5 = bf16[64,8192]{1,0:T(8,128)(2,1)} collective-permute-done((bf16[64,8192]{1,0:T(8,128)(2,1)S(1)}, bf16[64,8192]{1,0:T(8,128)(2,1)}, u32[]{:S(2)}, u32[]{:S(2)}) %collective-permute-start.5) | collective-permute-done | bytes 1048608 | tf_op jit(solution)/shard_map/ppermute | solution.py:34
  616.6 145.8 %all-reduce.8.cloned.1.call-done = f32[128,128]{1,0:T(8,128)} async-done(((f32[128,128]{1,0:T(8,128)}), f32[128,128]{1,0:T(8,128)}) %all-reduce.8.cloned.1.call-update) | async-done | bytes 65552 | tf_op jit(solution)/shard_map/psum | solution.py:69
  766.0 5.8 cholesky.215
  781.8 5.8 cholesky.226
  789.0 4.9 custom-call.38
  796.0 5.8 cholesky.237
  (189 shorter events, 97.7 us)
Async XLA Ops:
  7.2 2.2 copy-start.5
  7.2 267.8 %all-reduce.4.cloned.1.call-start = ((), (), s32[]{:S(2)}) async-start(), calls=%async_computation | async-start | bytes 131072 | tf_op jit(solution)/shard_map/psum | solution.py:69
  9.3 3.2 copy-start
  11.4 7.7 copy-start.11
  12.5 27.9 %collective-permute-start = (bf16[128,512]{0,1:T(8,128)(2,1)S(1)}, bf16[128,512]{0,1:T(8,128)(2,1)S(1)}, u32[]{:S(2)}, u32[]{:S(2)}) collective-permute-start(bf16[128,512]{0,1:T(8,128)(2,1)S(1)} %get-tuple-element.6), channel_id=1, source_target_pairs={{0,4},{4,8},{8,12},{12,16},{16,20},{20,24},{24,28},{28,32},{32,36}... | collective-permute-start | bytes 393224 | tf_op jit(solution)/shard_map/ppermute | solution.py:19
  17.1 23.3 %collective-permute-start.1 = (bf16[128,512]{0,1:T(8,128)(2,1)S(1)}, bf16[128,512]{0,1:T(8,128)(2,1)S(1)}, u32[]{:S(2)}, u32[]{:S(2)}) collective-permute-start(bf16[128,512]{0,1:T(8,128)(2,1)S(1)} %get-tuple-element.7), channel_id=1, source_target_pairs={{4,0},{8,4},{12,8},{16,12},{20,16},{24,20},{28,24},{32,28},{36,32}... | collective-permute-start | bytes 393224 | tf_op jit(solution)/shard_map/ppermute | solution.py:22
  100.3 417.0 %all-reduce.6.cloned.1.call-start = ((), (), s32[]{:S(2)}) async-start(), calls=%async_computation.1 | async-start | bytes 131072 | tf_op jit(solution)/shard_map/psum | solution.py:69
  275.0 31.8 %copy-start.4 = (f32[128,128]{1,0:T(8,128)S(1)}, f32[128,128]{1,0:T(8,128)}, u32[]{:S(2)}) copy-start(f32[128,128]{1,0:T(8,128)} %all-reduce.4.cloned.1.call-done) | copy-start | bytes 196612
  322.2 24.4 %collective-permute-start.2 = (bf16[64,8192]{1,0:T(8,128)(2,1)S(1)}, bf16[64,8192]{1,0:T(8,128)(2,1)S(1)}, u32[]{:S(2)}, u32[]{:S(2)}) collective-permute-start(bf16[64,8192]{1,0:T(8,128)(2,1)S(1)} %convolution_convert_fusion.3), channel_id=1, source_target_pairs={{0,1},{1,0},{2,3},{3,2},{4,5},{5,4},{6,7},{7,6},{8,9},{9,8},{10,11... | collective-permute-start | bytes 3145736 | tf_op jit(solution)/shard_map/ppermute | solution.py:34
  346.8 1.0 copy-start.6
  346.8 1.4 copy-start.8
  346.8 2.8 copy-start.1
  349.5 412.9 %all-reduce.8.cloned.1.call-start = ((), (), s32[]{:S(2)}) async-start(), calls=%async_computation.2 | async-start | bytes 131072 | tf_op jit(solution)/shard_map/psum | solution.py:69
  352.5 211.2 %copy-start.7 = (bf16[64,8192]{1,0:T(8,128)(2,1)S(1)}, bf16[64,8192]{1,0:T(8,128)(2,1)}, u32[]{:S(2)}) copy-start(bf16[64,8192]{1,0:T(8,128)(2,1)} %copy-done.6) | copy-start | bytes 3145732
  352.5 215.7 %collective-permute-start.4 = (bf16[64,8192]{1,0:T(8,128)(2,1)S(1)}, bf16[64,8192]{1,0:T(8,128)(2,1)}, u32[]{:S(2)}, u32[]{:S(2)}) collective-permute-start(bf16[64,8192]{1,0:T(8,128)(2,1)S(1)} %convolution_convert_fusion.1), channel_id=1, source_target_pairs={{0,1},{1,0},{2,3},{3,2},{4,5},{5,4},{6,7},{7,6},{8,9},{9,8},{10,11... | collective-permute-start | bytes 3145736 | tf_op jit(solution)/shard_map/ppermute | solution.py:34
  517.4 31.8 %copy-start.2 = (f32[128,128]{1,0:T(8,128)S(1)}, f32[128,128]{1,0:T(8,128)}, u32[]{:S(2)}) copy-start(f32[128,128]{1,0:T(8,128)} %all-reduce.6.cloned.1.call-done) | copy-start | bytes 196612
  565.4 25.9 %collective-permute-start.3 = (bf16[64,8192]{1,0:T(8,128)(2,1)S(1)}, bf16[64,8192]{1,0:T(8,128)(2,1)S(1)}, u32[]{:S(2)}, u32[]{:S(2)}) collective-permute-start(bf16[64,8192]{1,0:T(8,128)(2,1)S(1)} %convolution_convert_fusion.2), channel_id=1, source_target_pairs={{0,2},{2,0},{1,3},{3,1},{4,6},{6,4},{5,7},{7,5},{8,10},{10,8},{9,1... | collective-permute-start | bytes 3145736 | tf_op jit(solution)/shard_map/ppermute | solution.py:34
  570.1 22.8 %copy-start.10 = (bf16[64,8192]{1,0:T(8,128)(2,1)}, bf16[64,8192]{1,0:T(8,128)(2,1)S(1)}, u32[]{:S(2)}) copy-start(bf16[64,8192]{1,0:T(8,128)(2,1)S(1)} %convolution_convert_fusion) | copy-start | bytes 3145732
  570.1 43.8 %collective-permute-start.5 = (bf16[64,8192]{1,0:T(8,128)(2,1)S(1)}, bf16[64,8192]{1,0:T(8,128)(2,1)}, u32[]{:S(2)}, u32[]{:S(2)}) collective-permute-start(bf16[64,8192]{1,0:T(8,128)(2,1)S(1)} %convolution_convert_fusion), channel_id=1, source_target_pairs={{0,2},{2,0},{1,3},{3,1},{4,6},{6,4},{5,7},{7,5},{8,10},{10,8},{9,1... | collective-permute-start | bytes 3145736 | tf_op jit(solution)/shard_map/ppermute | solution.py:34
  762.4 31.8 %copy-start.3 = (f32[128,128]{1,0:T(8,128)S(1)}, f32[128,128]{1,0:T(8,128)}, u32[]{:S(2)}) copy-start(f32[128,128]{1,0:T(8,128)} %all-reduce.8.cloned.1.call-done) | copy-start | bytes 196612
  808.1 1.2 copy-start.9
Sparse Core Ops, SparseCore 0:
  100.5 174.4 all-reduce.3
  349.6 167.6 all-reduce.5
  593.0 169.3 all-reduce.7
where the time goes:
time: 826 us; the launch traced here: 817 us
  waiting for transfers between devices  549 us (66%)
  other arithmetic  122 us (15%)
  matrix products  59.5 us (7%)
  local copies, waits for them, and re-layouts  59.3 us (7%)
  between operations  14.8 us (2%)
  starting transfers between devices  12.9 us (2%)
    psum x3, waiting for transfers between devices, coefficients_of(): return compress(lax.psum(local_gram, 'space'))  484 us
    ppermute x4, waiting for transfers between devices, partner(): return lax.ppermute(block, axis, route)  64.9 us
    another operation x27, other arithmetic, compress(): jnp.linalg.cholesky(inner_gram / (scales[:, None] * scales[None, :]))  58.7 us
    another operation x18, other arithmetic, compress(): lax.linalg.triangular_solve(factor_lower, normed, left_side=False, lower=...  49.9 us
    dot_general x1, matrix products, weigh_rows(): jnp.einsum('cbkq,kqbr->cbr', picked, factor, preferred_element_type=jnp.f...  29 us
    gather x1, local copies, waits for them, and re-layouts, weigh_rows(): picked = jnp.take(blocks, local_index, axis=1)  22.8 us
    reshape x1, local copies, waits for them, and re-layouts, weigh_rows(): factor = mass_factor.reshape(NEIGHBOURS, BLOCK_DOFS, -1, BLOCK_DOFS)  20.9 us
  transfers between devices with their start and end apart: 9, of which 6 were waited for; matrix products, arithmetic and copies ran while one was open for 10% of the time, Pallas kernels for 0%

commit v1 on v0

v1 whole, which is shorter than its diff:
```python
import functools

import jax
import jax.numpy as jnp
from jax import lax
from jax.experimental import pallas as pl
from jax.experimental.pallas import tpu as pltpu
from jax.sharding import PartitionSpec as P

BLOCK = 64
RANK = 64
NEIGHBOURS = 7
REACH = 8
STEPS = 3
LOCAL_BLOCKS = 128
N_SPACE = 64
N_TM = 4
ROWS = 128
SLAB = LOCAL_BLOCKS * BLOCK
SHARE = SLAB // N_TM
HALO = REACH * BLOCK
WINDOW = SHARE + 2 * HALO
SHARE_BLOCKS = SHARE // BLOCK
TILES = WINDOW // 128
MESH = pl.DeviceIdType.MESH
HIGHEST = lax.Precision.HIGHEST
F32 = jnp.float32
BF16 = jnp.bfloat16


def dot_nn(a, b):
    return lax.dot_general(
        a, b, (((1,), (0,)), ((), ())), precision=HIGHEST, preferred_element_type=F32
    )


def dot_nt(a, b):
    return lax.dot_general(
        a, b, (((1,), (1,)), ((), ())), precision=HIGHEST, preferred_element_type=F32
    )


def span(target):
    low = max(0, SHARE * target - HALO)
    high = min(SLAB, SHARE * (target + 1) + HALO)
    return low, high - low, low - (SHARE * target - HALO)


def exchange_kernel(prior, snaps, out, bounce, send_sem, recv_sem, halo_send, halo_recv, local_sem):
    s = lax.axis_index("space")
    t = lax.axis_index("tm")
    up = lax.rem(s + 1, N_SPACE)
    down = lax.rem(s + N_SPACE - 1, N_SPACE)
    barrier = pltpu.get_barrier_semaphore()
    for g in range(N_TM):

        @pl.when(t != g)
        def _():
            pl.semaphore_signal(barrier, inc=1, device_id=(s, g), device_id_type=MESH)

        @pl.when(t == 0)
        def _():
            pl.semaphore_signal(barrier, inc=1, device_id=(down, g), device_id_type=MESH)

        @pl.when(t == N_TM - 1)
        def _():
            pl.semaphore_signal(barrier, inc=1, device_id=(up, g), device_id_type=MESH)

    pl.semaphore_wait(barrier, N_TM + 1)
    sources = (prior, snaps)

    def rows_of(group, part):
        return pl.ds(pl.multiple_of(group * ROWS + part * 64, 64), 64)

    def halo(part, side):
        low = SLAB - HALO if side == 0 else 0
        at = 0 if side == 0 else WINDOW - HALO
        return pltpu.make_async_remote_copy(
            src_ref=sources[part].at[:, pl.ds(low, HALO)],
            dst_ref=out.at[rows_of(t, part), pl.ds(at, HALO)],
            send_sem=halo_send.at[side, part],
            recv_sem=halo_recv.at[t, part],
            device_id=(up, 0) if side == 0 else (down, N_TM - 1),
            device_id_type=MESH,
        )

    def share(part, target):
        low, width, at = span(target)
        return pltpu.make_async_remote_copy(
            src_ref=sources[part].at[:, pl.ds(low, width)],
            dst_ref=out.at[rows_of(t, part), pl.ds(at, width)],
            send_sem=send_sem.at[target, part],
            recv_sem=recv_sem.at[t, part],
            device_id=(s, target),
            device_id_type=MESH,
        )

    def load(part, target):
        low, width, at = span(target)
        return pltpu.make_async_copy(
            sources[part].at[:, pl.ds(low, width)],
            bounce.at[pl.ds(part * 64, 64), pl.ds(at, width)],
            local_sem.at[part],
        )

    def store(part, target):
        low, width, at = span(target)
        return pltpu.make_async_copy(
            bounce.at[pl.ds(part * 64, 64), pl.ds(at, width)],
            out.at[pl.ds(target * ROWS + part * 64, 64), pl.ds(at, width)],
            local_sem.at[2 + part],
        )

    for own in range(N_TM):

        @pl.when(t == own)
        def _():
            for hop in (2, 1, 3):
                for part in range(2):
                    share(part, (own + hop) % N_TM).start()

    for part in range(2):
        for side in range(2):
            halo(part, side).start()
    for own in range(N_TM):

        @pl.when(t == own)
        def _():
            for part in range(2):
                load(part, own).start()
            for part in range(2):
                load(part, own).wait()
                store(part, own).start()
            for part in range(2):
                store(part, own).wait()
            low, width, at = span(own)
            for part in range(2):
                for hop in (1, 3, 2):
                    g = (own + hop) % N_TM
                    pltpu.make_async_remote_copy(
                        src_ref=sources[part].at[:, pl.ds(low, width)],
                        dst_ref=out.at[pl.ds(g * ROWS + part * 64, 64), pl.ds(at, width)],
                        send_sem=send_sem.at[own, part],
                        recv_sem=recv_sem.at[g, part],
                        device_id=(s, own),
                        device_id_type=MESH,
                    ).wait_recv()
                    share(part, g).wait_send()
            if own in (0, N_TM - 1):
                at = 0 if own == 0 else WINDOW - HALO
                for part in range(2):
                    for g in range(N_TM):
                        pltpu.make_async_remote_copy(
                            src_ref=sources[part].at[:, pl.ds(0, HALO)],
                            dst_ref=out.at[pl.ds(g * ROWS + part * 64, 64), pl.ds(at, HALO)],
                            send_sem=halo_send.at[0, part],
                            recv_sem=halo_recv.at[g, part],
                            device_id=(s, own),
                            device_id_type=MESH,
                        ).wait_recv()

    for part in range(2):
        for side in range(2):
            halo(part, side).wait_send()


def exchange(prior, snaps):
    return pl.pallas_call(
        exchange_kernel,
        out_shape=jax.ShapeDtypeStruct((N_TM * ROWS, WINDOW), BF16),
        in_specs=[pl.BlockSpec(memory_space=pl.ANY)] * 2,
        out_specs=pl.BlockSpec(memory_space=pl.ANY),
        scratch_shapes=[
            pltpu.VMEM((ROWS, WINDOW), BF16),
            pltpu.SemaphoreType.DMA((N_TM, 2)),
            pltpu.SemaphoreType.DMA((N_TM, 2)),
            pltpu.SemaphoreType.DMA((2, 2)),
            pltpu.SemaphoreType.DMA((N_TM, 2)),
            pltpu.SemaphoreType.DMA((4,)),
        ],
        compiler_params=pltpu.CompilerParams(collective_id=0, has_side_effects=True),
        name="exchange",
    )(prior, snaps)


def weigh_kernel(place, nb, x, mass, w, gram, shifted, factor, picked, sem):
    s, t = place[0], place[1]
    fetch = pltpu.make_async_copy(
        mass.at[:, :, pl.ds(pl.multiple_of(t * SHARE, 128), SHARE)], factor, sem
    )
    fetch.start()
    first = s * LOCAL_BLOCKS + t * SHARE_BLOCKS - REACH
    lane = lax.broadcasted_iota(jnp.int32, (1, 128), 1)
    in_low = lane < BLOCK
    for m in range(TILES + 1):
        before = x[:, pl.ds(128 * max(m - 1, 0), 128)]
        after = x[:, pl.ds(128 * min(m, TILES - 1), 128)]
        shifted[:, pl.ds(128 * m, 128)] = jnp.concatenate(
            [before[:, BLOCK:], after[:, :BLOCK]], axis=1
        )
    fetch.wait()

    def one_tile(j, carry):
        zero = jnp.zeros((BLOCK, 128), BF16)
        pieces = []
        for k in range(NEIGHBOURS):
            n_low = nb[(2 * j) * NEIGHBOURS + k] - first
            n_high = nb[(2 * j + 1) * NEIGHBOURS + k] - first
            odd_low = lax.rem(n_low, 2)
            odd_high = lax.rem(n_high, 2)
            low_at = pl.multiple_of(((n_low + 1) // 2) * 128, 128)
            high_at = pl.multiple_of((n_high // 2) * 128, 128)

            @pl.when(odd_low == 0)
            def _():
                picked[:, pl.ds(128 * k, 128)] = x[:, pl.ds(low_at, 128)]

            @pl.when(odd_low == 1)
            def _():
                picked[:, pl.ds(128 * k, 128)] = shifted[:, pl.ds(low_at, 128)]

            @pl.when(odd_high == 1)
            def _():
                picked[:, pl.ds(128 * k, 128)] = jnp.where(
                    in_low, picked[:, pl.ds(128 * k, 128)], x[:, pl.ds(high_at, 128)]
                )

            @pl.when(odd_high == 0)
            def _():
                picked[:, pl.ds(128 * k, 128)] = jnp.where(
                    in_low, picked[:, pl.ds(128 * k, 128)], shifted[:, pl.ds(high_at, 128)]
                )

            block = factor[k, :, pl.ds(pl.multiple_of(j * 128, 128), 128)]
            pieces.append(jnp.where(in_low, block, zero))
            pieces.append(jnp.where(in_low, zero, block))
        result = jnp.dot(
            picked[...], jnp.concatenate(pieces, axis=0), preferred_element_type=F32
        )
        w[:, pl.ds(pl.multiple_of(j * 128, 128), 128)] = result.astype(BF16)
        return carry

    lax.fori_loop(0, SHARE_BLOCKS // 2, one_tile, 0)
    at = 0
    for a in range(N_TM):
        for b in range(a, N_TM):
            gram[at] = lax.dot_general(
                w[pl.ds(a * ROWS, ROWS), :],
                w[pl.ds(b * ROWS, ROWS), :],
                (((1,), (1,)), ((), ())),
                preferred_element_type=F32,
            )
            at += 1


def weigh(place, nb, x, mass):
    rows = N_TM * ROWS
    return pl.pallas_call(
        weigh_kernel,
        out_shape=(
            jax.ShapeDtypeStruct((rows, SHARE), BF16),
            jax.ShapeDtypeStruct((10, ROWS, ROWS), F32),
        ),
        in_specs=[
            pl.BlockSpec(memory_space=pltpu.SMEM),
            pl.BlockSpec(memory_space=pltpu.SMEM),
            pl.BlockSpec(memory_space=pltpu.VMEM),
            pl.BlockSpec(memory_space=pl.ANY),
        ],
        out_specs=(
            pl.BlockSpec(memory_space=pltpu.VMEM),
            pl.BlockSpec(memory_space=pltpu.VMEM),
        ),
        scratch_shapes=[
            pltpu.VMEM((rows, (TILES + 1) * 128), BF16),
            pltpu.VMEM((NEIGHBOURS, BLOCK, SHARE), BF16),
            pltpu.VMEM((rows, NEIGHBOURS * 128), BF16),
            pltpu.SemaphoreType.DMA,
        ],
        name="weigh",
    )(place, nb, x, mass)


PIECE = 40


def reduce_kernel(inp, out, half, r_core, s_x, r_x, s_y, r_y, r_z, send_sem, recv_sem):
    s = lax.axis_index("space")
    x = lax.axis_index("tm")
    c = lax.rem(s, 2)
    y = lax.rem(s // 2, 4)
    z = s // 8

    def space_of(zz, yy, cc):
        return zz * 8 + yy * 2 + cc

    core_peer = (space_of(z, y, 1 - c), x)
    x_peers = [(s, lax.rem(x + d, 4)) for d in (1, 2, 3)]
    y_peers = [(space_of(z, lax.rem(y + d, 4), c), x) for d in (1, 2, 3)]
    z_peers = [(space_of(lax.rem(z + d, 8), y, c), x) for d in range(1, 8)]
    barrier = pltpu.get_barrier_semaphore()
    for peer in [core_peer] + x_peers + y_peers + z_peers:
        pl.semaphore_signal(barrier, inc=1, device_id=peer, device_id_type=MESH)
    pl.semaphore_wait(barrier, 14)

    def copy(src, dst, slot, peer):
        return pltpu.make_async_remote_copy(
            src_ref=src,
            dst_ref=dst,
            send_sem=send_sem.at[slot],
            recv_sem=recv_sem.at[slot],
            device_id=peer,
            device_id_type=MESH,
        )

    def run(copies):
        for one in copies:
            one.start()
        for one in copies:
            one.wait()

    run([copy(inp.at[1 - c], r_core, 0, core_peer)])
    half[...] = inp[c] + r_core[...]
    run(
        [
            copy(half.at[lax.rem(x + d, 4)], r_x.at[d - 1], d, x_peers[d - 1])
            for d in (2, 1, 3)
        ]
    )
    s_x[...] = half[x] + r_x[0] + r_x[1] + r_x[2]
    run(
        [
            copy(s_x.at[lax.rem(y + d, 4)], r_y.at[d - 1], 3 + d, y_peers[d - 1])
            for d in (2, 1, 3)
        ]
    )
    r_z[z] = s_x[y] + r_y[0] + r_y[1] + r_y[2]
    run([copy(r_z.at[z], r_z.at[z], 6 + d, z_peers[d - 1]) for d in (4, 3, 5, 2, 6, 1, 7)])
    total = r_z[0]
    for i in range(1, 8):
        total = total + r_z[i]
    out[c, x, y] = total
    run([copy(out.at[c, x, y], out.at[c, x, y], 13 + d, y_peers[d - 1]) for d in (2, 1, 3)])
    run([copy(out.at[c, x], out.at[c, x], 16 + d, x_peers[d - 1]) for d in (2, 1, 3)])
    run([copy(out.at[c], out.at[c], 20, core_peer)])


def all_reduce(gram):
    shape = (2, 4, 4, PIECE, 128)
    return pl.pallas_call(
        reduce_kernel,
        out_shape=jax.ShapeDtypeStruct(shape, F32),
        in_specs=[pl.BlockSpec(memory_space=pltpu.VMEM)],
        out_specs=pl.BlockSpec(memory_space=pltpu.VMEM),
        scratch_shapes=[
            pltpu.VMEM(shape[1:], F32),
            pltpu.VMEM(shape[1:], F32),
            pltpu.VMEM(shape[2:], F32),
            pltpu.VMEM((3,) + shape[2:], F32),
            pltpu.VMEM((1, PIECE, 128), F32),
            pltpu.VMEM((3, PIECE, 128), F32),
            pltpu.VMEM((8, PIECE, 128), F32),
            pltpu.SemaphoreType.DMA((21,)),
            pltpu.SemaphoreType.DMA((21,)),
        ],
        compiler_params=pltpu.CompilerParams(collective_id=1, has_side_effects=True),
        name="all_reduce",
    )(gram.reshape(shape)).reshape(10, ROWS, ROWS)


def eliminate(inners):
    sub = lax.broadcasted_iota(jnp.int32, (8, 128), 0)
    lane = lax.broadcasted_iota(jnp.int32, (8, 128), 1)
    grids = []
    for inner in inners:
        tiles = []
        for i in range(8):
            unit = jnp.where(lane == 8 * i + sub + BLOCK, 1.0, 0.0).astype(F32)
            left = jnp.concatenate([inner[8 * i : 8 * i + 8, :], jnp.zeros((8, BLOCK), F32)], axis=1)
            tiles.append(left + unit)
        grids.append(tiles)
    roots = [[] for _ in inners]
    for j in range(BLOCK):
        here, inside = divmod(j, 8)
        for tiles, root in zip(grids, roots):
            cols = [
                jnp.broadcast_to(tiles[i][:, j : j + 1], (8, 128)) for i in range(here, 8)
            ]
            pivot = jnp.broadcast_to(cols[0][inside : inside + 1, :], (8, 128))
            row = jnp.broadcast_to(tiles[here][inside : inside + 1, :], (8, 128)) * (1.0 / pivot)
            if inside == 0:
                root.append(pivot)
            else:
                root[here] = jnp.where(sub == inside, pivot, root[here])
            for i in range(here, 8):
                change = cols[i - here] * row
                if i == here:
                    change = jnp.where(sub > inside, change, 0.0)
                tiles[i] = tiles[i] - change
    return [
        jnp.concatenate([tile * lax.rsqrt(d) for tile, d in zip(tiles, root)], axis=0)
        for tiles, root in zip(grids, roots)
    ]


def compress(grams):
    rows = [gram[:RANK, :] for gram in grams]
    products = rows
    zeros = jnp.zeros((BLOCK, ROWS), F32)

    def step(products):
        seconds = [dot_nn(p, g) for p, g in zip(products, grams)]
        inners = [dot_nt(p, q) for p, q in zip(products, seconds)]
        inverses = eliminate(inners)
        nexts = [
            dot_nn(inv, jnp.concatenate([zeros, q], axis=0)) for inv, q in zip(inverses, seconds)
        ]
        return inverses, nexts

    for _ in range(STEPS - 1):
        _, products = step(products)
    inverses, nexts = step(products)
    result = []
    for inv, p, q in zip(inverses, products, nexts):
        weights = dot_nn(inv, jnp.concatenate([zeros, p], axis=0))
        lengths = jnp.sqrt(jnp.sum(q * q, axis=1, keepdims=True) + 1e-06)
        result.append((weights * lengths).astype(BF16).astype(F32))
    return result


def merge_kernel(gram, out, full, below, middle, above):
    index = {}
    for a in range(N_TM):
        for b in range(a, N_TM):
            index[a, b] = len(index)
    for (a, b), at in index.items():
        block = gram[at]
        full[pl.ds(a * ROWS, ROWS), pl.ds(b * ROWS, ROWS)] = block
        if a != b:
            full[pl.ds(b * ROWS, ROWS), pl.ds(a * ROWS, ROWS)] = block.T
    below[...] = jnp.zeros_like(below)
    above[...] = jnp.zeros_like(above)
    lowest = compress([gram[index[g, g]] for g in range(N_TM)])
    for g in range(N_TM):
        below[pl.ds(g * RANK, RANK), pl.ds(g * ROWS, ROWS)] = lowest[g]
    for p in range(2):
        half = [
            dot_nn(lowest[g], full[pl.ds(g * ROWS, ROWS), pl.ds(2 * p * ROWS, 2 * ROWS)])
            for g in range(N_TM)
        ]
        middle[:, pl.ds(p * ROWS, ROWS)] = dot_nt(
            jnp.concatenate(half, axis=0),
            below[pl.ds(2 * p * RANK, 2 * RANK), pl.ds(2 * p * ROWS, 2 * ROWS)],
        )
    second = compress([middle[pl.ds(p * ROWS, ROWS), pl.ds(p * ROWS, ROWS)] for p in range(2)])
    for p in range(2):
        above[pl.ds(p * RANK, RANK), pl.ds(p * ROWS, ROWS)] = second[p]
    half = [dot_nn(second[p], middle[pl.ds(p * ROWS, ROWS), :]) for p in range(2)]
    last = compress([dot_nt(jnp.concatenate(half, axis=0), above[...])])[0]
    out[...] = dot_nn(dot_nn(last, above[...]), below[...]).astype(BF16)


def merge(gram):
    return pl.pallas_call(
        merge_kernel,
        out_shape=jax.ShapeDtypeStruct((RANK, N_TM * ROWS), BF16),
        in_specs=[pl.BlockSpec(memory_space=pltpu.VMEM)],
        out_specs=pl.BlockSpec(memory_space=pltpu.VMEM),
        scratch_shapes=[
            pltpu.VMEM((N_TM * ROWS, N_TM * ROWS), F32),
            pltpu.VMEM((N_TM * RANK, N_TM * ROWS), F32),
            pltpu.VMEM((N_TM * RANK, N_TM * RANK), F32),
            pltpu.VMEM((2 * RANK, 2 * ROWS), F32),
        ],
        name="merge",
    )(gram)


def shards(snapshots, prior_basis, mass_factor, neighbours):
    s = lax.axis_index("space")
    t = lax.axis_index("tm")
    place = jnp.stack([s, t]).astype(jnp.int32)
    nb = lax.dynamic_slice_in_dim(neighbours, t * SHARE_BLOCKS, SHARE_BLOCKS, 0).reshape(-1)
    x = exchange(prior_basis, snapshots)
    w, gram = weigh(place, nb, x, mass_factor)
    coefficients = merge(all_reduce(gram))
    own = lax.slice_in_dim(x, HALO, HALO + SHARE, axis=1)
    basis = jnp.dot(coefficients, own, preferred_element_type=F32).astype(BF16)
    weighted = jnp.dot(coefficients, w, preferred_element_type=F32).astype(BF16)
    return basis, weighted


def solution(mesh):
    return jax.shard_map(
        shards,
        mesh=mesh,
        in_specs=(P("tm", "space"), P("tm", "space"), P(None, None, "space"), P("space", None)),
        out_specs=(P(None, ("space", "tm")), P(None, ("space", "tm"))),
        check_vma=False,
    )
```

time: 826 us -> 193 us (0.23); the launches traced: 817 us -> 193 us
  waiting for transfers between devices: 549 us -> 0 us
  Pallas kernels: 0 us -> 188 us
  other arithmetic: 122 us -> 0.59 us
  local copies, waits for them, and re-layouts: 59.3 us -> 0.93 us
  matrix products: 59.5 us -> 3.37 us
  between operations: 14.8 us -> 0.68 us
  starting transfers between devices: 12.9 us -> 0 us
    psum x3 -> x0, waiting for transfers between devices: 484 us -> none  [coefficients_of(): return compress(lax.psum(local_gram, 'space'))]
    pallas_call x0 -> x4, Pallas kernels: none -> 188 us  [the longest x1 86.6 us: merge(): pl.pallas_call(merge_kernel, out_shape=jax.ShapeDtypeStruct((RANK, N_TM *...]
    another operation x45 -> x1, other arithmetic: 109 us -> 0.59 us  [shards(): place = jnp.stack([s, t]).astype(jnp.int32)]
    ppermute x6 -> x0, waiting for transfers between devices: 65 us -> none  [the longest x4 64.9 us: partner(): return lax.ppermute(block, axis, route)]
    dot_general x40 -> x2, matrix products: 57 us -> 3.37 us  [the longest x1 2.18 us: shards(): basis = jnp.dot(coefficients, own, preferred_element_type=F32).astype(BF16)]
    gather x10 -> x0, local copies, waits for them, and re-layouts: 30.1 us -> none  [the longest x1 22.8 us: weigh_rows(): picked = jnp.take(blocks, local_index, axis=1)]
    reshape x1, local copies, waits for them, and re-layouts: 20.9 us -> 0.67 us  [shards(): lax.dynamic_slice_in_dim(neighbours, t * SHARE_BLOCKS, SHARE_BLOCKS, 0)]
    ppermute x6 -> x0, starting transfers between devices: 12.8 us -> none  [the longest x4 6.28 us: partner(): return lax.ppermute(block, axis, route)]
  transfers between devices with their start and end apart: 9 -> 0, of which waited for: 6 -> 0; matrix products, arithmetic and copies ran while one was open for 10% -> 0% of each run, Pallas kernels for 0% -> 0%
where the time goes in v1:
time: 193 us
  Pallas kernels  188 us (97%)
  matrix products  3.37 us (2%)
    pallas_call x1, Pallas kernels, merge(): pl.pallas_call(merge_kernel, out_shape=jax.ShapeDtypeStruct((RANK, N_TM *...  86.6 us
    pallas_call x1, Pallas kernels, exchange(): pl.pallas_call(exchange_kernel, out_shape=jax.ShapeDtypeStruct((N_TM * RO...  41.3 us
    pallas_call x1, Pallas kernels, all_reduce(): pl.pallas_call(reduce_kernel, out_shape=jax.ShapeDtypeStruct(shape, F32),...  36.2 us
    pallas_call x1, Pallas kernels, weigh(): pl.pallas_call(weigh_kernel, out_shape=(jax.ShapeDtypeStruct((rows, SHARE...  23.4 us

profile of v1, /device:TPU:1, one launch (start us, length us, event | category | flops | bytes accessed | tf_op | source)
XLA Modules:
  0.0 193.1 jit_solution(6376661476531064854)
XLA Ops:
  0.6 0.0 copy-start
  0.6 0.6 pad_add_fusion.place
  1.2 0.1 copy-done
  1.3 0.1 constant_dynamic-slice_fusion
  1.4 0.1 copy.6
  1.5 0.7 reshape.13.nb
  2.2 41.3 %exchange.1.x = bf16[512,3072]{1,0:T(8,128)(2,1)} custom-call(bf16[64,8192]{1,0:T(8,128)(2,1)} %prior.1, bf16[64,8192]{1,0:T(8,128)(2,1)} %snaps.1), custom_call_target="tpu_custom_call" | custom-call | tf_op jit(solution)/shard_map/exchange/pallas_call | solution.py:168
  43.5 0.0 copy-start.1
  43.5 23.4 %weigh.1 = (bf16[512,2048]{1,0:T(8,128)(2,1)}, f32[10,128,128]{2,1,0:T(8,128)}) custom-call(s32[2]{0:T(128)} %pad_add_fusion.place, s32[224]{0:T(256)} %reshape.13.nb, bf16[512,3072]{1,0:T(8,128)(2,1)} %exchange.1.x, bf16[7,64,8192]{2,1,0:T(8,128)(2,1)} %mass.1), custom_call_target="tpu_custom_call" | custom-call | tf_op jit(solution)/shard_map/weigh/pallas_call | solution.py:258
  67.0 36.2 %all_reduce.1 = f32[2,4,4,40,128]{4,3,2,1,0:T(8,128)} custom-call(f32[2,4,4,40,128]{4,3,2,1,0:T(8,128)} %bitcast.8), custom_call_target="tpu_custom_call" | custom-call | tf_op jit(solution)/shard_map/all_reduce/pallas_call | solution.py:350
  103.2 86.6 %merge.1 = bf16[64,512]{1,0:T(8,128)(2,1)} custom-call(f32[10,128,128]{2,1,0:T(8,128)} %bitcast.7), custom_call_target="tpu_custom_call" | custom-call | tf_op jit(solution)/shard_map/merge/pallas_call | solution.py:464
  189.7 0.0 copy-done.1
  189.7 0.0 copy-start.2
  189.7 0.0 copy-start.3
  189.7 2.2 %convolution_convert_fusion.1 = bf16[64,2048]{1,0:T(8,128)(2,1)} fusion(bf16[64,512]{1,0:T(8,128)(2,1)} %merge.1, bf16[512,3072]{1,0:T(8,128)(2,1)S(1)} %copy-done.1), kind=kOutput, calls=%fused_computation.1 | convolution fusion | flops 134348800 | bytes 2424832 | tf_op jit(solution)/shard_map/dot_general | solution.py:488
  191.9 0.0 copy-done.2
  191.9 0.0 copy-done.3
  191.9 1.2 convolution_convert_fusion
Async XLA Ops:
  0.6 0.7 copy-start
  43.5 146.2 %copy-start.1 = (bf16[512,3072]{1,0:T(8,128)(2,1)S(1)}, bf16[512,3072]{1,0:T(8,128)(2,1)}, u32[]{:S(2)}) copy-start(bf16[512,3072]{1,0:T(8,128)(2,1)} %exchange.1.x) | copy-start | bytes 9437188
  189.7 2.2 %copy-start.2 = (bf16[512,2048]{1,0:T(8,128)(2,1)S(1)}, bf16[512,2048]{1,0:T(8,128)(2,1)}, u32[]{:S(2)}) copy-start(bf16[512,2048]{1,0:T(8,128)(2,1)} %get-tuple-element.5) | copy-start | bytes 6291460
  189.7 2.2 %copy-start.3 = (bf16[64,512]{1,0:T(8,128)(2,1)S(1)}, bf16[64,512]{1,0:T(8,128)(2,1)}, u32[]{:S(2)}) copy-start(bf16[64,512]{1,0:T(8,128)(2,1)} %merge.1) | copy-start | bytes 196612

commit v2 on v1

--- a/solution.py
+++ b/solution.py
@@ -183,64 +183,50 @@
     )(prior, snaps)
 
 
-def weigh_kernel(place, nb, x, mass, w, gram, shifted, factor, picked, sem):
+def pick_tile(nb, first, j, wide, width, factor, in_low):
+    zero = jnp.zeros((BLOCK, 128), BF16)
+    picks, pieces = [], []
+    for k in range(NEIGHBOURS):
+        low = nb[2 * j * NEIGHBOURS + k] - first
+        high = nb[(2 * j + 1) * NEIGHBOURS + k] - first
+        low_at = ((low + 1) >> 1) * 128 + (low & 1) * width
+        high_at = (high >> 1) * 128 + (1 - (high & 1)) * width
+        picks.append(
+            jnp.where(
+                in_low,
+                wide[:, pl.ds(pl.multiple_of(low_at, 128), 128)],
+                wide[:, pl.ds(pl.multiple_of(high_at, 128), 128)],
+            )
+        )
+        block = factor[k, :, pl.ds(pl.multiple_of(j * 128, 128), 128)]
+        pieces += [jnp.where(in_low, block, zero), jnp.where(in_low, zero, block)]
+    return jnp.concatenate(picks, axis=1), jnp.concatenate(pieces, axis=0)
+
+
+def weigh_kernel(place, nb, x, mass, w, gram, wide, factor, sem):
     s, t = place[0], place[1]
     fetch = pltpu.make_async_copy(
         mass.at[:, :, pl.ds(pl.multiple_of(t * SHARE, 128), SHARE)], factor, sem
     )
     fetch.start()
     first = s * LOCAL_BLOCKS + t * SHARE_BLOCKS - REACH
-    lane = lax.broadcasted_iota(jnp.int32, (1, 128), 1)
-    in_low = lane < BLOCK
+    in_low = lax.broadcasted_iota(jnp.int32, (1, 128), 1) < BLOCK
+    wide[:, pl.ds(0, WINDOW)] = x[...]
     for m in range(TILES + 1):
         before = x[:, pl.ds(128 * max(m - 1, 0), 128)]
         after = x[:, pl.ds(128 * min(m, TILES - 1), 128)]
-        shifted[:, pl.ds(128 * m, 128)] = jnp.concatenate(
+        wide[:, pl.ds(WINDOW + 128 * m, 128)] = jnp.concatenate(
             [before[:, BLOCK:], after[:, :BLOCK]], axis=1
         )
     fetch.wait()
 
     def one_tile(j, carry):
-        zero = jnp.zeros((BLOCK, 128), BF16)
-        pieces = []
-        for k in range(NEIGHBOURS):
-            n_low = nb[(2 * j) * NEIGHBOURS + k] - first
-            n_high = nb[(2 * j + 1) * NEIGHBOURS + k] - first
-            odd_low = lax.rem(n_low, 2)
-            odd_high = lax.rem(n_high, 2)
-            low_at = pl.multiple_of(((n_low + 1) // 2) * 128, 128)
-            high_at = pl.multiple_of((n_high // 2) * 128, 128)
-
-            @pl.when(odd_low == 0)
-            def _():
-                picked[:, pl.ds(128 * k, 128)] = x[:, pl.ds(low_at, 128)]
-
-            @pl.when(odd_low == 1)
-            def _():
-                picked[:, pl.ds(128 * k, 128)] = shifted[:, pl.ds(low_at, 128)]
-
-            @pl.when(odd_high == 1)
-            def _():
-                picked[:, pl.ds(128 * k, 128)] = jnp.where(
-                    in_low, picked[:, pl.ds(128 * k, 128)], x[:, pl.ds(high_at, 128)]
-                )
-
-            @pl.when(odd_high == 0)
-            def _():
-                picked[:, pl.ds(128 * k, 128)] = jnp.where(
-                    in_low, picked[:, pl.ds(128 * k, 128)], shifted[:, pl.ds(high_at, 128)]
-                )
-
-            block = factor[k, :, pl.ds(pl.multiple_of(j * 128, 128), 128)]
-            pieces.append(jnp.where(in_low, block, zero))
-            pieces.append(jnp.where(in_low, zero, block))
-        result = jnp.dot(
-            picked[...], jnp.concatenate(pieces, axis=0), preferred_element_type=F32
-        )
+        modes, rows = pick_tile(nb, first, j, wide, WINDOW, factor, in_low)
+        result = jnp.dot(modes, rows, preferred_element_type=F32)
         w[:, pl.ds(pl.multiple_of(j * 128, 128), 128)] = result.astype(BF16)
         return carry
 
-    lax.fori_loop(0, SHARE_BLOCKS // 2, one_tile, 0)
+    lax.fori_loop(0, SHARE_BLOCKS // 2, one_tile, 0, unroll=4)
     at = 0
     for a in range(N_TM):
         for b in range(a, N_TM):
@@ -272,9 +258,8 @@
             pl.BlockSpec(memory_space=pltpu.VMEM),
         ),
         scratch_shapes=[
-            pltpu.VMEM((rows, (TILES + 1) * 128), BF16),
+            pltpu.VMEM((rows, (2 * TILES + 1) * 128), BF16),
             pltpu.VMEM((NEIGHBOURS, BLOCK, SHARE), BF16),
-            pltpu.VMEM((rows, NEIGHBOURS * 128), BF16),
             pltpu.SemaphoreType.DMA,
         ],
         name="weigh",
@@ -379,28 +364,31 @@
             left = jnp.concatenate([inner[8 * i : 8 * i + 8, :], jnp.zeros((8, BLOCK), F32)], axis=1)
             tiles.append(left + unit)
         grids.append(tiles)
-    roots = [[] for _ in inners]
-    for j in range(BLOCK):
-        here, inside = divmod(j, 8)
-        for tiles, root in zip(grids, roots):
-            cols = [
-                jnp.broadcast_to(tiles[i][:, j : j + 1], (8, 128)) for i in range(here, 8)
-            ]
-            pivot = jnp.broadcast_to(cols[0][inside : inside + 1, :], (8, 128))
-            row = jnp.broadcast_to(tiles[here][inside : inside + 1, :], (8, 128)) * (1.0 / pivot)
-            if inside == 0:
-                root.append(pivot)
-            else:
-                root[here] = jnp.where(sub == inside, pivot, root[here])
-            for i in range(here, 8):
-                change = cols[i - here] * row
-                if i == here:
-                    change = jnp.where(sub > inside, change, 0.0)
-                tiles[i] = tiles[i] - change
-    return [
-        jnp.concatenate([tile * lax.rsqrt(d) for tile, d in zip(tiles, root)], axis=0)
-        for tiles, root in zip(grids, roots)
-    ]
+    outs = [[] for _ in inners]
+    for p in range(8):
+        panels = [
+            [[jnp.broadcast_to(tiles[i][:, 8 * p + q : 8 * p + q + 1], (8, 128)) for q in range(8)] for i in range(p, 8)]
+            for tiles in grids
+        ]
+        roots = [jnp.ones((8, 128), F32) for _ in grids]
+        for q in range(8):
+            for m, (tiles, cols) in enumerate(zip(grids, panels)):
+                pivot = jnp.broadcast_to(cols[0][q][q : q + 1, :], (8, 128))
+                inv = 1.0 / pivot
+                roots[m] = jnp.where(sub == q, pivot, roots[m])
+                for r in range(q + 1, 8):
+                    factor = jnp.broadcast_to(cols[0][r][q : q + 1, :], (8, 128)) * inv
+                    for i in range(8 - p):
+                        cols[i][r] = cols[i][r] - cols[i][q] * factor
+                row = jnp.broadcast_to(tiles[p][q : q + 1, :], (8, 128)) * inv
+                for i in range(p, 8):
+                    change = cols[i - p][q] * row
+                    if i == p:
+                        change = jnp.where(sub > q, change, 0.0)
+                    tiles[i] = tiles[i] - change
+        for out, tiles, root in zip(outs, grids, roots):
+            out.append(tiles[p] * lax.rsqrt(root))
+    return [jnp.concatenate(out, axis=0) for out in outs]
 
 
 def compress(grams):

time: 193 us -> 126 us (0.65)
  Pallas kernels: 188 us -> 120 us
    pallas_call x1, Pallas kernels: 86.6 us -> 31.2 us  [merge(): pl.pallas_call(merge_kernel, out_shape=jax.ShapeDtypeStruct((RANK, N_TM *...]
    pallas_call x1, Pallas kernels: 23.4 us -> 11.7 us  [weigh(): pl.pallas_call(weigh_kernel, out_shape=(jax.ShapeDtypeStruct((rows, SHARE...]
where the time goes in v2:
time: 126 us
  Pallas kernels  120 us (95%)
  matrix products  3.37 us (3%)
    pallas_call x1, Pallas kernels, exchange(): pl.pallas_call(exchange_kernel, out_shape=jax.ShapeDtypeStruct((N_TM * RO...  41.3 us
    pallas_call x1, Pallas kernels, all_reduce(): pl.pallas_call(reduce_kernel, out_shape=jax.ShapeDtypeStruct(shape, F32),...  36.1 us
    pallas_call x1, Pallas kernels, merge(): pl.pallas_call(merge_kernel, out_shape=jax.ShapeDtypeStruct((RANK, N_TM *...  31.2 us
    pallas_call x1, Pallas kernels, weigh(): pl.pallas_call(weigh_kernel, out_shape=(jax.ShapeDtypeStruct((rows, SHARE...  11.7 us

profile of v2, /device:TPU:1, one launch (start us, length us, event | category | flops | bytes accessed | tf_op | source)
XLA Modules:
  0.0 125.8 jit_solution(6460653346211385296)
XLA Ops:
  0.6 0.0 copy-start
  0.6 0.6 pad_add_fusion.place
  1.2 0.1 copy-done
  1.3 0.1 constant_dynamic-slice_fusion
  1.4 0.1 copy.6
  1.5 0.7 reshape.13.nb
  2.2 41.3 %exchange.1.x = bf16[512,3072]{1,0:T(8,128)(2,1)} custom-call(bf16[64,8192]{1,0:T(8,128)(2,1)} %prior.1, bf16[64,8192]{1,0:T(8,128)(2,1)} %snaps.1), custom_call_target="tpu_custom_call" | custom-call | tf_op jit(solution)/shard_map/exchange/pallas_call | solution.py:168
  43.5 0.0 copy-start.1
  43.5 11.7 %weigh.1 = (bf16[512,2048]{1,0:T(8,128)(2,1)}, f32[10,128,128]{2,1,0:T(8,128)}) custom-call(s32[2]{0:T(128)} %pad_add_fusion.place, s32[224]{0:T(256)} %reshape.13.nb, bf16[512,3072]{1,0:T(8,128)(2,1)} %exchange.1.x, bf16[7,64,8192]{2,1,0:T(8,128)(2,1)} %mass.1), custom_call_target="tpu_custom_call" | custom-call | tf_op jit(solution)/shard_map/weigh/pallas_call | solution.py:244
  55.2 36.1 %all_reduce.1 = f32[2,4,4,40,128]{4,3,2,1,0:T(8,128)} custom-call(f32[2,4,4,40,128]{4,3,2,1,0:T(8,128)} %bitcast.8), custom_call_target="tpu_custom_call" | custom-call | tf_op jit(solution)/shard_map/all_reduce/pallas_call | solution.py:335
  91.3 31.2 %merge.1 = bf16[64,512]{1,0:T(8,128)(2,1)} custom-call(f32[10,128,128]{2,1,0:T(8,128)} %bitcast.7), custom_call_target="tpu_custom_call" | custom-call | tf_op jit(solution)/shard_map/merge/pallas_call | solution.py:452
  122.4 0.0 copy-done.1
  122.4 0.0 copy-start.2
  122.5 0.0 copy-start.3
  122.5 2.2 %convolution_convert_fusion.1 = bf16[64,2048]{1,0:T(8,128)(2,1)} fusion(bf16[64,512]{1,0:T(8,128)(2,1)} %merge.1, bf16[512,3072]{1,0:T(8,128)(2,1)S(1)} %copy-done.1), kind=kOutput, calls=%fused_computation.1 | convolution fusion | flops 134348800 | bytes 2424832 | tf_op jit(solution)/shard_map/dot_general | solution.py:476
  124.6 0.0 copy-done.2
  124.6 0.0 copy-done.3
  124.6 1.2 convolution_convert_fusion
Async XLA Ops:
  0.6 0.7 copy-start
  43.5 78.9 %copy-start.1 = (bf16[512,3072]{1,0:T(8,128)(2,1)S(1)}, bf16[512,3072]{1,0:T(8,128)(2,1)}, u32[]{:S(2)}) copy-start(bf16[512,3072]{1,0:T(8,128)(2,1)} %exchange.1.x) | copy-start | bytes 9437188
  122.4 2.2 %copy-start.2 = (bf16[512,2048]{1,0:T(8,128)(2,1)S(1)}, bf16[512,2048]{1,0:T(8,128)(2,1)}, u32[]{:S(2)}) copy-start(bf16[512,2048]{1,0:T(8,128)(2,1)} %get-tuple-element.5) | copy-start | bytes 6291460
  122.5 2.2 %copy-start.3 = (bf16[64,512]{1,0:T(8,128)(2,1)S(1)}, bf16[64,512]{1,0:T(8,128)(2,1)}, u32[]{:S(2)}) copy-start(bf16[64,512]{1,0:T(8,128)(2,1)} %merge.1) | copy-start | bytes 196612
